TPU v7x, 32 devices: a whole 2x2x4 slice. The times are simulated.
32 devices in a mesh: ens: 2 (over y), space: 4 (over z), tm: 2 (over x), mom: 2 (over core).
Axes of the slice: x: 2, y: 2, z: 4, core: 2. Of those that a mesh axis runs over, the one named last changes fastest.
Arguments:
- eigvecs: bfloat16 [8, 2, 3, 256, 2048], P(('ens', 'tm'), None, None, None, 'space'), parts along dimension 0, may hold values from -0.359375 to 0.359375
- momenta: int32 [4, 3], P('mom'), may hold values from 1 to 2
- pairs: int32 [2, 2], replicated, may hold values from 0 to 3, as said below
- spin_weights: float32 [4, 4], replicated, may hold values from -1 to 1
- perambulators: bfloat16 [4, 2, 4, 4, 256, 256], P(('ens', 'tm'), None, None, None, 'space'), parts along dimension 0, may hold values from -0.0234375 to 0.0234375
Outputs:
- blocks: bfloat16 [4, 4, 2, 256, 256], P(('ens', 'tm'), 'mom', None, 'space'), parts along dimension 0
There are 2 independent parts, one for each index of `ens`. A program takes and returns all parts, laid end to end along the dimension named above; an argument that names none is the same for every part. Nothing has to cross between parts.
Inputs may be any that keep to these rules, and one draw needn't show every extreme that they name: pairs[q, 0], the sink, lies in time group q: (q) * 2 <= pairs[q, 0] < (q + 1) * 2; pairs[q, 1], the source, is any timeslice.
All inputs are finite; a program needn't handle non-finite values.
Results may differ from a plain program's by a relative error of at most 0.008.
Values may be sent and summed in bfloat16 or wider, within the bound.
No kernel may reach another device: no remote copies, remote signals or barrier semaphores. Data moves between devices by JAX's collectives and lax.ppermute only.
A program may use at most 64 MiB of HBM per device.

v0:
```python
import math
import jax
import jax.numpy as jnp
from jax import lax
from jax.sharding import PartitionSpec as P

LAT = 48
EXACT_PRECISION = lax.Precision.HIGHEST


def phases(momenta, site_ids):
    xcoord = (site_ids % LAT).astype(jnp.float32)
    ycoord = (site_ids // LAT % LAT).astype(jnp.float32)
    zcoord = (site_ids // (LAT * LAT)).astype(jnp.float32)
    mom_float = momenta.astype(jnp.float32)
    angles = (
        mom_float[:, 0:1] * xcoord + mom_float[:, 1:2] * ycoord + mom_float[:, 2:3] * zcoord
    ) * (2.0 * math.pi / LAT)
    return (jnp.cos(angles), jnp.sin(angles))


def elemental_terms(eigvecs, cosine_rows, sine_rows):
    contract_dims = (((0, 2), (0, 2)), ((), ()))
    per_time = []
    for which_time in range(eigvecs.shape[0]):
        real_vec = eigvecs[which_time, 0]
        imag_vec = eigvecs[which_time, 1]
        real_wide = real_vec.astype(jnp.float32)
        imag_wide = imag_vec.astype(jnp.float32)
        per_mom = []
        for which_mom in range(cosine_rows.shape[0]):
            cosine = cosine_rows[which_mom]
            sine = sine_rows[which_mom]
            real_turned = (cosine * real_wide + sine * imag_wide).astype(jnp.bfloat16)
            imag_turned = (cosine * imag_wide - sine * real_wide).astype(jnp.bfloat16)
            real_part = lax.dot_general(
                real_vec, real_turned, contract_dims, preferred_element_type=jnp.float32
            ) + lax.dot_general(
                imag_vec, imag_turned, contract_dims, preferred_element_type=jnp.float32
            )
            imag_part = lax.dot_general(
                real_vec, imag_turned, contract_dims, preferred_element_type=jnp.float32
            ) - lax.dot_general(
                imag_vec, real_turned, contract_dims, preferred_element_type=jnp.float32
            )
            per_mom.append(jnp.stack([real_part, imag_part]))
        per_time.append(jnp.stack(per_mom))
    return jnp.stack(per_time)


def source_slots(held_rows, pairs, my_group, times_dev, tm_size, pair_dev):
    wanted = pairs[:, 1].reshape(tm_size, pair_dev)
    local_times = jnp.arange(times_dev, dtype=jnp.int32) + my_group * times_dev
    chosen = (wanted[:, :, None] == local_times).astype(jnp.bfloat16)
    return jnp.einsum(
        "rqt,tmcij->rqmcij", chosen, held_rows, preferred_element_type=jnp.float32
    ).astype(jnp.bfloat16)


def sink_select(held_rows, my_pairs, my_group, times_dev):
    local_times = jnp.arange(times_dev, dtype=jnp.int32) + my_group * times_dev
    chosen = (my_pairs[:, 0][:, None] == local_times).astype(jnp.bfloat16)
    return jnp.einsum(
        "qt,tmcij->qmcij", chosen, held_rows, preferred_element_type=jnp.float32
    ).astype(jnp.bfloat16)


def bridge(mixed_block, source):
    real_part = jnp.einsum(
        "qkl,qmjl->qmkj", mixed_block[:, 0], source[:, :, 0], preferred_element_type=jnp.float32
    ) + jnp.einsum(
        "qkl,qmjl->qmkj", mixed_block[:, 1], source[:, :, 1], preferred_element_type=jnp.float32
    )
    imag_part = jnp.einsum(
        "qkl,qmjl->qmkj", mixed_block[:, 1], source[:, :, 0], preferred_element_type=jnp.float32
    ) - jnp.einsum(
        "qkl,qmjl->qmkj", mixed_block[:, 0], source[:, :, 1], preferred_element_type=jnp.float32
    )
    return jnp.stack([real_part, imag_part], 2).astype(jnp.bfloat16)


def attach(sink_elem, bridged):
    real_part = jnp.einsum(
        "qmik,qmkj->qmij", sink_elem[:, :, 0], bridged[:, :, 0], preferred_element_type=jnp.float32
    ) - jnp.einsum(
        "qmik,qmkj->qmij", sink_elem[:, :, 1], bridged[:, :, 1], preferred_element_type=jnp.float32
    )
    imag_part = jnp.einsum(
        "qmik,qmkj->qmij", sink_elem[:, :, 0], bridged[:, :, 1], preferred_element_type=jnp.float32
    ) + jnp.einsum(
        "qmik,qmkj->qmij", sink_elem[:, :, 1], bridged[:, :, 0], preferred_element_type=jnp.float32
    )
    return jnp.stack([real_part, imag_part], 2)


def local(eigvecs, momenta, pairs, spin_weights, perambulators):
    times_dev = eigvecs.shape[0]
    vec_count = eigvecs.shape[3]
    sites_dev = eigvecs.shape[4]
    pair_dev = perambulators.shape[0]
    tm_size = lax.axis_size("tm")
    space_size = lax.axis_size("space")
    my_group = lax.axis_index("tm")
    my_place = lax.axis_index("space")
    rows_dev = vec_count // space_size
    row_first = my_place * rows_dev
    site_ids = my_place * sites_dev + jnp.arange(sites_dev, dtype=jnp.int32)
    cosine_rows, sine_rows = phases(momenta, site_ids)
    partial_value = elemental_terms(eigvecs, cosine_rows, sine_rows)
    my_pairs = lax.dynamic_slice_in_dim(pairs, my_group * pair_dev, pair_dev, 0)
    whole = lax.psum(partial_value, "space").astype(jnp.bfloat16)
    outgoing = source_slots(whole, pairs, my_group, times_dev, tm_size, pair_dev)
    arrived = lax.all_to_all(outgoing, "tm", split_axis=0, concat_axis=0, tiled=True)
    source_full = jnp.sum(arrived, axis=0, dtype=jnp.float32).astype(jnp.bfloat16)
    sink_whole = sink_select(whole, my_pairs, my_group, times_dev)
    sink_own = lax.dynamic_slice_in_dim(sink_whole, row_first, rows_dev, 3)
    mixed_peramb = jnp.einsum(
        "ab,qcabkl->qckl",
        spin_weights,
        perambulators.astype(jnp.float32),
        precision=EXACT_PRECISION,
    ).astype(jnp.bfloat16)
    bridged = bridge(lax.all_gather(mixed_peramb, "space", axis=2, tiled=True), source_full)
    blocks = attach(sink_own, bridged).astype(jnp.bfloat16)
    return blocks


def solution(mesh):
    return jax.shard_map(
        local,
        mesh=mesh,
        in_specs=(
            P(("ens", "tm"), None, None, None, "space"),
            P("mom", None),
            P(),
            P(),
            P(("ens", "tm"), None, None, None, "space", None),
        ),
        out_specs=P(("ens", "tm"), "mom", None, "space", None),
        check_vma=False,
    )
```

profile of v0, /device:TPU:0, one launch (start us, length us, event | category | flops | bytes accessed | tf_op | source)
XLA Modules:
  0.0 120.1 jit_solution(8111220607492806430)
XLA Ops:
  0.0 0.0 copy-start
  0.0 0.8 convert_element_type.166
  0.8 0.2 slice_reduce_fusion.3
  1.0 0.1 fusion.149
  1.1 0.1 sin.3
  1.3 0.0 copy-start.1
  1.3 2.2 %convolution_bitcast_fusion.14 = f32[256,256]{1,0:T(8,128)S(1)} fusion(f32[512]{0:T(512)S(1)} %bitcast.288, f32[512]{0:T(512)S(1)} %bitcast.296, bf16[2,2,3,256,512]{4,3,2,1,0:T(8,128)(2,1)} %param.5), kind=kOutput, calls=%fused_computation.55 | convolution fusion | flops 203685888 | bytes 2625536 | tf_op jit(solution)/shard_map/dot_general | solution.py:38
  3.5 0.4 copy-done.1
  3.9 0.4 convolution_bitcast_fusion.12
  4.3 0.5 convolution_bitcast_fusion.10
  4.8 0.4 convolution_bitcast_fusion.8
  5.2 0.4 convolution_bitcast_fusion.6
  5.7 0.5 convolution_bitcast_fusion.4
  6.1 0.5 convolution_bitcast_fusion.2
  6.6 0.4 convolution_bitcast_fusion
  7.1 0.4 fusion.22
  7.5 0.5 fusion.24
  8.0 0.5 fusion.26
  8.4 0.5 fusion.28
  8.9 0.5 fusion.30
  9.4 0.5 fusion.32
  9.8 0.5 fusion.34
  10.3 0.5 fusion.36
  10.8 0.1 maximum_bitcast_fusion
  11.0 0.1 maximum_bitcast_fusion.1
  11.1 0.1 pad_maximum_fusion
  11.2 79.3 %all-reduce.1 = bf16[2,2,2,256,256]{3,4,2,1,0:T(8,128)(2,1)} all-reduce(f32[2,2,2,256,256]{3,4,2,1,0:T(8,128)S(1)} %pad_maximum_fusion), channel_id=1, replica_groups=mesh['ens'=2,'space'=4,'tm'=2,'mom'=2] {'space'}, use_global_device_ids=true, to_apply=%region_0.1 | all-reduce | flops 524288 | bytes 3145728 | tf_op jit(solution)/shard_map/psum | solution.py:111
  90.5 2.5 %copy.12 = bf16[2,2,2,256,256]{4,0,3,2,1:T(2,128)(2,1)S(1)} copy(bf16[2,2,2,256,256]{3,4,2,1,0:T(8,128)(2,1)} %all-reduce.1) | data formatting | bytes 2097152 | tf_op jit(solution)/shard_map/convert_element_type | solution.py:111
  93.1 0.0 copy-done.3
  93.1 0.2 slice_reduce_fusion
  93.3 1.3 %fusion.16 = bf16[2,1,2,2,256,256]{5,0,4,3,2,1:T(2,128)(2,1)S(1)} fusion(bf16[2,2,2,256,256]{4,0,3,2,1:T(2,128)(2,1)S(1)} %copy.12, s32[2]{0:T(128)S(1)} %iota_add_fusion.1, s32[2]{0:T(128)S(1)} %slice_reduce_fusion), kind=kOutput, calls=%fused_computation.34 | convolution fusion | flops 2621444 | bytes 2097168 | tf_op jit(solution)/shard_map/rqt,tmcij->rqmcij/dot_general | solution.py:55
  94.6 1.1 copy.13
  95.7 3.9 %all-to-all-start = ((bf16[2,1,2,2,256,256]{5,4,3,2,1,0:T(8,128)(2,1)}), bf16[2,1,2,2,256,256]{5,4,3,2,1,0:T(8,128)(2,1)S(1)}, u32[]{:S(2)}, u32[]{:S(2)}) async-start(bf16[2,1,2,2,256,256]{5,4,3,2,1,0:T(8,128)(2,1)} %copy.13), calls=%async_computation | async-start | bytes 2097152 | tf_op jit(solution)/shard_map/all_to_all | solution.py:113
  99.6 2.1 %fusion.41 = bf16[1,2,64,256,1]{3,0,4,2,1:T(2,128)(2,1)S(1)} fusion(f32[4,4,1,1,1]{1,2,0,4,3:T(1,128)S(1)} %bitcast.304, bf16[2,4,4,64,256]{4,3,2,1,0:T(8,128)(2,1)S(1)} %bitcast.261), kind=kOutput, calls=%fused_computation.82 | convolution fusion | flops 6291456 | bytes 1114176 | tf_op jit(solution)/shard_map/ab,qcabkl->qckl/dot_general | solution.py:117
  101.8 1.3 %fusion.145 = bf16[1,2,2,256,256]{4,0,3,2,1:T(2,128)(2,1)S(1)} fusion(bf16[2,2,2,256,256]{4,0,3,2,1:T(2,128)(2,1)S(1)} %copy.12, s32[]{:T(128)S(1)} %bitcast.305, s32[]{:T(128)S(6)} %mul.205), kind=kOutput, calls=%fused_computation.194 | convolution fusion | flops 1048580 | bytes 1572872 | tf_op jit(solution)/shard_map/qt,tmcij->qmcij/dot_general | solution.py:63
  103.0 0.1 copy.37
  103.1 13.8 %all-gather = bf16[2,256,256]{2,1,0:T(8,128)(2,1)S(1)} all-gather(bf16[2,64,256]{2,1,0:T(8,128)(2,1)S(1)} %bitcast.271), channel_id=2, replica_groups=mesh['ens'=2,'space'=4,'tm'=2,'mom'=2] {'space'}, dimensions={1}, use_global_device_ids=true | all-gather | bytes 327680 | tf_op jit(solution)/shard_map/all_gather | solution.py:123
  116.9 0.0 all-to-all-done
  116.9 0.5 reduce_sum.14
  117.5 0.2 fusion.100
  117.7 0.3 fusion.99
  118.0 0.3 fusion.20
  118.3 0.3 fusion.19
  118.5 0.2 fusion.135
  118.7 0.2 fusion.134
  118.9 0.2 fusion.40
  119.2 0.2 fusion.39
  119.4 0.7 copy.20
  (18 shorter events, 0.3 us)
Async XLA Ops:
  0.0 99.6 %copy-start = (bf16[1,2,4,4,64,256]{5,4,3,2,1,0:T(8,128)(2,1)S(1)}, bf16[1,2,4,4,64,256]{5,4,3,2,1,0:T(8,128)(2,1)}, u32[]{:S(2)}) copy-start(bf16[1,2,4,4,64,256]{5,4,3,2,1,0:T(8,128)(2,1)} %param.9) | copy-start | bytes 3145732
  1.3 2.6 %copy-start.1 = (bf16[2,2,3,256,512]{4,3,2,1,0:T(8,128)(2,1)S(1)}, bf16[2,2,3,256,512]{4,3,2,1,0:T(8,128)(2,1)}, u32[]{:S(2)}) copy-start(bf16[2,2,3,256,512]{4,3,2,1,0:T(8,128)(2,1)} %param.5) | copy-start | bytes 9437188
  90.5 2.6 %copy-start.3 = (s32[2,2]{1,0:T(2,128)S(1)}, s32[2,2]{1,0:T(2,128)}, u32[]{:S(2)}) copy-start(s32[2,2]{1,0:T(2,128)} %param.7) | copy-start | bytes 52
  95.7 3.9 %copy-start.2 = (f32[4,4]{1,0:T(4,128)S(1)}, f32[4,4]{1,0:T(4,128)}, u32[]{:S(2)}) copy-start(f32[4,4]{1,0:T(4,128)} %param.8) | copy-start | bytes 196
  95.7 21.2 %all-to-all-start = ((bf16[2,1,2,2,256,256]{5,4,3,2,1,0:T(8,128)(2,1)}), bf16[2,1,2,2,256,256]{5,4,3,2,1,0:T(8,128)(2,1)S(1)}, u32[]{:S(2)}, u32[]{:S(2)}) async-start(bf16[2,1,2,2,256,256]{5,4,3,2,1,0:T(8,128)(2,1)} %copy.13), calls=%async_computation | async-start | bytes 2097152 | tf_op jit(solution)/shard_map/all_to_all | solution.py:113
where the time goes:
time: 120 us
  blocking collectives  93.1 us (78%)
  matrix products  15.5 us (13%)
  local copies, waits for them, and re-layouts  5.32 us (4%)
  starting transfers between devices  3.89 us (3%)
  other arithmetic  1.86 us (2%)
    psum x1, blocking collectives, local(): whole = lax.psum(partial_value, 'space').astype(jnp.bfloat16)  79.3 us
    all_gather x1, blocking collectives, local(): lax.all_gather(mixed_peramb, 'space', axis=2, tiled=True)  13.8 us
    all_to_all x1, starting transfers between devices, local(): lax.all_to_all(outgoing, 'tm', split_axis=0, concat_axis=0, tiled=True)  3.89 us
    dot_general x4, matrix products, elemental_terms(): lax.dot_general(imag_vec, imag_turned, contract_dims, preferred_element_t...  3.57 us
    convert_element_type x1, local copies, waits for them, and re-layouts, local(): whole = lax.psum(partial_value, 'space').astype(jnp.bfloat16)  2.54 us
  transfers between devices with their start and end apart: 1, of which 0 were waited for; matrix products, arithmetic and copies ran while one was open for 3% of the time, Pallas kernels for 0%

commit v1 on v0

--- a/solution.py
+++ b/solution.py
@@ -6,6 +6,28 @@
 
 LAT = 48
 EXACT_PRECISION = lax.Precision.HIGHEST
+
+
+def joined_along(pieces, dim):
+    pieces = jnp.moveaxis(pieces, 0, dim)
+    shape = pieces.shape
+    return pieces.reshape(*shape[:dim], shape[dim] * shape[dim + 1], *shape[dim + 2 :])
+
+
+def doubled(array, axis):
+    size = lax.axis_size(axis)
+    blocks = array[None]
+    for level in range(size.bit_length() - 1):
+        bit = 1 << level
+        other = lax.ppermute(blocks, axis, [(i, i ^ bit) for i in range(size)])
+        both = jnp.stack([blocks, other])
+        upper = lax.axis_index(axis) >> level & 1
+        blocks = jnp.where(upper == 0, both, both[::-1]).reshape(-1, *array.shape)
+    return blocks
+
+
+def doubled_up(value, axis, dim):
+    return joined_along(doubled(value, axis), dim)
 
 
 def phases(momenta, site_ids):
@@ -120,7 +142,7 @@
         perambulators.astype(jnp.float32),
         precision=EXACT_PRECISION,
     ).astype(jnp.bfloat16)
-    bridged = bridge(lax.all_gather(mixed_peramb, "space", axis=2, tiled=True), source_full)
+    bridged = bridge(doubled_up(mixed_peramb, "space", 2), source_full)
     blocks = attach(sink_own, bridged).astype(jnp.bfloat16)
     return blocks
 

time: 120 us -> 117 us (0.975)
  blocking collectives: 93.1 us -> 79.3 us
  waiting for transfers between devices: 0.01 us -> 4.76 us
  starting transfers between devices: 3.89 us -> 5.89 us
  local copies, waits for them, and re-layouts: 5.32 us -> 7.05 us
  matrix products: 15.5 us -> 16.8 us
    all_gather x1 -> x0, blocking collectives: 13.8 us -> none  [local(): lax.all_gather(mixed_peramb, 'space', axis=2, tiled=True)]
    ppermute x0 -> x2, waiting for transfers between devices: none -> 4.76 us  [doubled(): other = lax.ppermute(blocks, axis, [(i, i ^ bit) for i in range(size)])]
    ppermute x0 -> x2, starting transfers between devices: none -> 2 us  [doubled(): other = lax.ppermute(blocks, axis, [(i, i ^ bit) for i in range(size)])]
    dot_general x1, matrix products: 1.27 us -> 2.49 us  [sink_select(): jnp.einsum('qt,tmcij->qmcij', chosen, held_rows, preferred_element_type=j...]
  transfers between devices with their start and end apart: 1 -> 3, of which waited for: 0 -> 2; matrix products, arithmetic and copies ran while one was open for 3% -> 6% of each run, Pallas kernels for 0% -> 0%
where the time goes in v1:
time: 117 us; the launch traced here: 116 us
  blocking collectives  79.3 us (68%)
  matrix products  16.8 us (14%)
  local copies, waits for them, and re-layouts  7.05 us (6%)
  starting transfers between devices  5.89 us (5%)
  waiting for transfers between devices  4.76 us (4%)
  other arithmetic  1.99 us (2%)
    psum x1, blocking collectives, local(): whole = lax.psum(partial_value, 'space').astype(jnp.bfloat16)  79.3 us
    ppermute x2, waiting for transfers between devices, doubled(): other = lax.ppermute(blocks, axis, [(i, i ^ bit) for i in range(size)])  4.76 us
    all_to_all x1, starting transfers between devices, local(): lax.all_to_all(outgoing, 'tm', split_axis=0, concat_axis=0, tiled=True)  3.89 us
    dot_general x4, matrix products, elemental_terms(): lax.dot_general(imag_vec, imag_turned, contract_dims, preferred_element_t...  3.57 us
    convert_element_type x1, local copies, waits for them, and re-layouts, local(): whole = lax.psum(partial_value, 'space').astype(jnp.bfloat16)  2.54 us
    dot_general x1, matrix products, sink_select(): jnp.einsum('qt,tmcij->qmcij', chosen, held_rows, preferred_element_type=j...  2.49 us
  transfers between devices with their start and end apart: 3, of which 2 were waited for; matrix products, arithmetic and copies ran while one was open for 6% of the time, Pallas kernels for 0%

profile of v1, /device:TPU:0, one launch (start us, length us, event | category | flops | bytes accessed | tf_op | source)
XLA Modules:
  0.0 116.2 jit_solution(13250775792741348487)
XLA Ops:
  0.0 0.8 convert_element_type.164
  0.8 0.2 slice_reduce_fusion.3
  1.0 0.1 fusion.153
  1.1 0.1 sin.3
  1.3 2.2 %convolution_bitcast_fusion.14 = f32[256,256]{1,0:T(8,128)S(1)} fusion(f32[512]{0:T(512)S(1)} %bitcast.314, f32[512]{0:T(512)S(1)} %bitcast.322, bf16[2,2,3,256,512]{4,3,2,1,0:T(8,128)(2,1)} %param.5), kind=kOutput, calls=%fused_computation.55 | convolution fusion | flops 203685888 | bytes 2625536 | tf_op jit(solution)/shard_map/dot_general | solution.py:60
  3.5 0.4 copy-done.2
  3.9 0.4 convolution_bitcast_fusion.12
  4.3 0.5 convolution_bitcast_fusion.10
  4.8 0.5 convolution_bitcast_fusion.8
  5.2 0.5 convolution_bitcast_fusion.6
  5.7 0.5 convolution_bitcast_fusion.4
  6.1 0.5 convolution_bitcast_fusion.2
  6.6 0.5 convolution_bitcast_fusion
  7.1 0.5 fusion.22
  7.5 0.5 fusion.24
  8.0 0.5 fusion.26
  8.4 0.5 fusion.28
  8.9 0.5 fusion.30
  9.4 0.5 fusion.32
  9.8 0.5 fusion.34
  10.3 0.5 fusion.36
  10.9 0.1 maximum_bitcast_fusion
  11.0 0.1 maximum_bitcast_fusion.1
  11.1 0.1 pad_maximum_fusion
  11.3 79.3 %all-reduce.1 = bf16[2,2,2,256,256]{3,4,2,1,0:T(8,128)(2,1)} all-reduce(f32[2,2,2,256,256]{3,4,2,1,0:T(8,128)S(1)} %pad_maximum_fusion), channel_id=1, replica_groups=mesh['ens'=2,'space'=4,'tm'=2,'mom'=2] {'space'}, use_global_device_ids=true, to_apply=%region_0.1 | all-reduce | flops 524288 | bytes 3145728 | tf_op jit(solution)/shard_map/psum | solution.py:133
  90.5 2.5 %copy.14 = bf16[2,2,2,256,256]{4,0,3,2,1:T(2,128)(2,1)S(1)} copy(bf16[2,2,2,256,256]{3,4,2,1,0:T(8,128)(2,1)} %all-reduce.1) | data formatting | bytes 2097152 | tf_op jit(solution)/shard_map/convert_element_type | solution.py:133
  93.1 0.2 slice_reduce_fusion
  93.3 1.3 %fusion.16 = bf16[2,1,2,2,256,256]{5,0,4,3,2,1:T(2,128)(2,1)S(1)} fusion(bf16[2,2,2,256,256]{4,0,3,2,1:T(2,128)(2,1)S(1)} %copy.14, s32[2]{0:T(128)S(1)} %iota_add_fusion.1, s32[2]{0:T(128)S(1)} %slice_reduce_fusion), kind=kOutput, calls=%fused_computation.34 | convolution fusion | flops 2621444 | bytes 2097168 | tf_op jit(solution)/shard_map/rqt,tmcij->rqmcij/dot_general | solution.py:77
  94.6 1.1 copy.15
  95.7 3.9 %all-to-all-start = ((bf16[2,1,2,2,256,256]{5,4,3,2,1,0:T(8,128)(2,1)}), bf16[2,1,2,2,256,256]{5,4,3,2,1,0:T(8,128)(2,1)S(1)}, u32[]{:S(2)}, u32[]{:S(2)}) async-start(bf16[2,1,2,2,256,256]{5,4,3,2,1,0:T(8,128)(2,1)} %copy.15), calls=%async_computation | async-start | bytes 2097152 | tf_op jit(solution)/shard_map/all_to_all | solution.py:135
  99.7 2.1 %fusion.41 = bf16[1,2,64,256,1]{3,0,4,2,1:T(2,128)(2,1)S(1)} fusion(f32[4,4,1,1,1]{1,2,0,4,3:T(1,128)S(1)} %bitcast.330, bf16[2,4,4,64,256]{4,3,2,1,0:T(8,128)(2,1)S(1)} %bitcast.284), kind=kOutput, calls=%fused_computation.82 | convolution fusion | flops 6291456 | bytes 1114176 | tf_op jit(solution)/shard_map/ab,qcabkl->qckl/dot_general | solution.py:139
  101.8 0.1 collective-permute-start
  101.9 4.3 %collective-permute-done = bf16[1,1,2,64,256]{4,3,2,1,0:T(8,128)(2,1)S(1)} collective-permute-done((bf16[1,1,2,64,256]{4,3,2,1,0:T(8,128)(2,1)S(1)}, bf16[1,1,2,64,256]{4,3,2,1,0:T(8,128)(2,1)S(1)}, u32[]{:S(2)}, u32[]{:S(2)}) %collective-permute-start) | collective-permute-done | bytes 65568 | tf_op jit(solution)/shard_map/ppermute | solution.py:22
  106.3 1.9 %collective-permute-start.1 = (bf16[2,1,2,64,256]{4,3,0,2,1:T(8,128)(2,1)S(1)}, bf16[2,1,2,64,256]{4,3,0,2,1:T(8,128)(2,1)S(1)}, u32[]{:S(2)}, u32[]{:S(2)}) collective-permute-start(bf16[2,1,2,64,256]{4,3,0,2,1:T(8,128)(2,1)S(1)} %get-tuple-element.11), channel_id=1, source_target_pairs={{0,8},{4,12},{8,0},{12,4},{1,9},{5,13},{9,1},{13,5},{2,10},{6,14},... | collective-permute-start | bytes 393224 | tf_op jit(solution)/shard_map/ppermute | solution.py:22
  108.2 2.5 %fusion.149 = bf16[1,2,2,256,256]{4,0,3,2,1:T(2,128)(2,1)S(1)} fusion(bf16[2,2,2,256,256]{4,0,3,2,1:T(2,128)(2,1)} %copy-done.1, s32[]{:T(128)S(1)} %bitcast.331, s32[]{:T(128)S(6)} %mul.205), kind=kOutput, calls=%fused_computation.202 | convolution fusion | flops 1048580 | bytes 1572872 | tf_op jit(solution)/shard_map/qt,tmcij->qmcij/dot_general | solution.py:85
  110.7 0.9 copy.45
  111.6 0.9 fusion.133
  112.5 0.4 collective-permute-done.1
  113.1 0.5 reduce_sum.14
  113.6 0.2 fusion.100
  113.8 0.3 fusion.99
  114.1 0.3 fusion.20
  114.4 0.3 fusion.19
  114.6 0.2 fusion.137
  114.8 0.2 fusion.136
  115.0 0.2 fusion.40
  115.3 0.2 fusion.39
  115.5 0.7 copy.24
  (27 shorter events, 0.4 us)
Async XLA Ops:
  0.0 99.6 %copy-start = (bf16[1,2,4,4,64,256]{5,4,3,2,1,0:T(8,128)(2,1)S(1)}, bf16[1,2,4,4,64,256]{5,4,3,2,1,0:T(8,128)(2,1)}, u32[]{:S(2)}) copy-start(bf16[1,2,4,4,64,256]{5,4,3,2,1,0:T(8,128)(2,1)} %param.9) | copy-start | bytes 3145732
  1.3 2.6 %copy-start.2 = (bf16[2,2,3,256,512]{4,3,2,1,0:T(8,128)(2,1)S(1)}, bf16[2,2,3,256,512]{4,3,2,1,0:T(8,128)(2,1)}, u32[]{:S(2)}) copy-start(bf16[2,2,3,256,512]{4,3,2,1,0:T(8,128)(2,1)} %param.5) | copy-start | bytes 9437188
  90.5 2.6 %copy-start.4 = (s32[2,2]{1,0:T(2,128)S(1)}, s32[2,2]{1,0:T(2,128)}, u32[]{:S(2)}) copy-start(s32[2,2]{1,0:T(2,128)} %param.7) | copy-start | bytes 52
  93.1 1.5 %copy-start.1 = (bf16[2,2,2,256,256]{4,0,3,2,1:T(2,128)(2,1)}, bf16[2,2,2,256,256]{4,0,3,2,1:T(2,128)(2,1)S(1)}, u32[]{:S(2)}) copy-start(bf16[2,2,2,256,256]{4,0,3,2,1:T(2,128)(2,1)S(1)} %copy.14) | copy-start | bytes 3145732
  95.7 3.9 %copy-start.3 = (f32[4,4]{1,0:T(4,128)S(1)}, f32[4,4]{1,0:T(4,128)}, u32[]{:S(2)}) copy-start(f32[4,4]{1,0:T(4,128)} %param.8) | copy-start | bytes 196
  95.7 17.3 %all-to-all-start = ((bf16[2,1,2,2,256,256]{5,4,3,2,1,0:T(8,128)(2,1)}), bf16[2,1,2,2,256,256]{5,4,3,2,1,0:T(8,128)(2,1)S(1)}, u32[]{:S(2)}, u32[]{:S(2)}) async-start(bf16[2,1,2,2,256,256]{5,4,3,2,1,0:T(8,128)(2,1)} %copy.15), calls=%async_computation | async-start | bytes 2097152 | tf_op jit(solution)/shard_map/all_to_all | solution.py:135
  101.8 4.4 %collective-permute-start = (bf16[1,1,2,64,256]{4,3,2,1,0:T(8,128)(2,1)S(1)}, bf16[1,1,2,64,256]{4,3,2,1,0:T(8,128)(2,1)S(1)}, u32[]{:S(2)}, u32[]{:S(2)}) collective-permute-start(bf16[1,1,2,64,256]{4,3,2,1,0:T(8,128)(2,1)S(1)} %bitcast.294), channel_id=1, source_target_pairs={{0,4},{4,0},{8,12},{12,8},{1,5},{5,1},{9,13},{13,9},{2,6},{6,2},{1... | collective-permute-start | bytes 196616 | tf_op jit(solution)/shard_map/ppermute | solution.py:22
  106.3 6.7 %collective-permute-start.1 = (bf16[2,1,2,64,256]{4,3,0,2,1:T(8,128)(2,1)S(1)}, bf16[2,1,2,64,256]{4,3,0,2,1:T(8,128)(2,1)S(1)}, u32[]{:S(2)}, u32[]{:S(2)}) collective-permute-start(bf16[2,1,2,64,256]{4,3,0,2,1:T(8,128)(2,1)S(1)} %get-tuple-element.11), channel_id=1, source_target_pairs={{0,8},{4,12},{8,0},{12,4},{1,9},{5,13},{9,1},{13,5},{2,10},{6,14},... | collective-permute-start | bytes 393224 | tf_op jit(solution)/shard_map/ppermute | solution.py:22
